TPU v7x, 512 devices: a whole 4x4x16 slice. The times are simulated.
512 devices in a mesh: ctx: 64 (over x, z), fsdp: 8 (over y, core).
Axes of the slice: x: 4, y: 4, z: 16, core: 2. Of those that a mesh axis runs over, the one named last changes fastest.
Arguments:
- tokens: bfloat16 [8, 8192, 4096], P('fsdp', 'ctx'), may hold values from -6 to 6
- queries: bfloat16 [8, 8192, 512], P('fsdp', 'ctx'), may hold values from -6 to 6
- flags: int32 [8, 8192], P('fsdp', 'ctx'), may hold values from 0 to 1, as said below
- w_key: bfloat16 [4096, 512], P(('ctx', 'fsdp')), may hold values from -0.09375 to 0.09375
- w_value: bfloat16 [4096, 512], P(('ctx', 'fsdp')), may hold values from -0.09375 to 0.09375
- norm_gain: float32 [512], replicated, may hold values from 0.25 to 1.75
Outputs:
- attended: bfloat16 [8, 8192, 512], P('fsdp', 'ctx')
Inputs may be any that keep to these rules, and one draw needn't show every extreme that they name: `flags`: in each sequence a document starts at token 0 and at every token k * 2048 + 2048 // 2; other tokens start one at random, never before token 3072 and never at the first token of a block. No document is longer than 2048 tokens.
All inputs are finite; a program needn't handle non-finite values.
Results may differ from a plain program's by a relative error of at most 0.0053.
Values may be sent and summed in bfloat16 or wider, within the bound.
A program may use at most 64 MiB of HBM per device.

v0:
```python
import jax
import jax.numpy as jnp
from jax import lax
from jax.sharding import PartitionSpec as P

HEAD = 128


def entering(array, axis, join, neutral):
    place = lax.axis_index(axis)
    gathered = jax.tree.map(
        lambda a, kind: lax.all_gather(a.astype(kind), axis), array, (jnp.bfloat16, jnp.bfloat16)
    )
    state = jax.tree.map(lambda a, e: jnp.zeros_like(a) + jnp.asarray(e, a.dtype), array, neutral)

    def one(lap, state):
        return join(
            state,
            jax.tree.map(
                lambda a, own: lax.dynamic_index_in_dim(a, lap, 0, False).astype(own.dtype),
                gathered,
                array,
            ),
        )

    return lax.fori_loop(0, place, one, state)


def feature(u):
    return jax.nn.elu(u) + 1.0


def combine(earlier, later):
    keep = 1.0 - later[0][0]
    return (jnp.maximum(earlier[0], later[0]), later[1] + keep * earlier[1])


def on_device(tokens, queries, flags, w_key, w_value, norm_gain):
    rows = tokens[0]
    count = rows.shape[0]
    width = w_key.shape[1]
    heads = width // HEAD
    full_panels = (
        lax.all_gather(w_key, ("ctx", "fsdp"), axis=0, tiled=True),
        lax.all_gather(w_value, ("ctx", "fsdp"), axis=0, tiled=True),
    )
    proj_key = jnp.dot(rows, full_panels[0], preferred_element_type=jnp.float32)
    proj_value = jnp.dot(rows, full_panels[1], preferred_element_type=jnp.float32)
    key = feature(proj_key).astype(jnp.bfloat16).reshape(count, heads, HEAD)
    value = proj_value.astype(jnp.bfloat16).reshape(count, heads, HEAD)
    query = feature(queries[0].astype(jnp.float32)).astype(jnp.bfloat16).reshape(count, heads, HEAD)
    seg = jnp.cumsum(flags[0])
    last = seg[count - 1]
    reset = (last > 0).astype(jnp.float32).reshape(1)
    tail = (seg == last).astype(jnp.bfloat16)
    local_state = jnp.einsum(
        "the,thf->hef", key * tail[:, None, None], value, preferred_element_type=jnp.float32
    )
    identity = (jnp.zeros((1,), jnp.float32), jnp.zeros_like(local_state))
    carried = entering((reset, local_state), "ctx", combine, identity)
    carried_b = carried[1].astype(jnp.bfloat16)
    places = jnp.arange(count, dtype=jnp.int32)
    allowed = (places[None, :] <= places[:, None]) & (seg[None, :] == seg[:, None])
    scores = jnp.einsum("the,she->hts", query, key, preferred_element_type=jnp.float32)
    scores = jnp.where(allowed[None, :, :], scores, 0.0).astype(jnp.bfloat16)
    inside = jnp.einsum("hts,shf->thf", scores, value, preferred_element_type=jnp.float32)
    first = (seg == 0).astype(jnp.float32)
    carried_term = (
        jnp.einsum("the,hef->thf", query, carried_b, preferred_element_type=jnp.float32)
        * first[:, None, None]
    )
    mixed = carried_term + inside
    scale = lax.rsqrt(jnp.mean(mixed * mixed, axis=-1, keepdims=True) + 1e-06)
    attended = (mixed * scale * norm_gain.reshape(heads, HEAD)).astype(jnp.bfloat16)
    return attended.reshape(1, count, width)


def solution(mesh):
    in_specs = (
        P("fsdp", "ctx", None),
        P("fsdp", "ctx", None),
        P("fsdp", "ctx"),
        P(("ctx", "fsdp"), None),
        P(("ctx", "fsdp"), None),
        P(),
    )
    out_specs = P("fsdp", "ctx", None)
    return jax.shard_map(
        on_device, mesh=mesh, in_specs=in_specs, out_specs=out_specs, check_vma=False
    )
```

profile of v0, /device:TPU:486, one launch (start us, length us, event | category | flops | bytes accessed | tf_op | source)
XLA Modules:
  0.0 710.5 jit_solution(16022774016434404635)
XLA Ops:
  10.1 196.2 %all-gather.7.cloned.1.call-done = bf16[4096,512]{1,0:T(8,128)(2,1)} async-done(((bf16[8,512]{1,0:T(8,128)(2,1)}), bf16[4096,512]{1,0:T(8,128)(2,1)}) %all-gather.7.cloned.1.call-update) | async-done | bytes 4194320 | tf_op jit(solution)/shard_map/all_gather | solution.py:45
  206.4 2.9 convolution_convert_fusion
  209.4 195.0 %all-gather.5.cloned.1.call-done = bf16[4096,512]{1,0:T(8,128)(2,1)} async-done(((bf16[8,512]{1,0:T(8,128)(2,1)}), bf16[4096,512]{1,0:T(8,128)(2,1)}) %all-gather.5.cloned.1.call-update) | async-done | bytes 4194320 | tf_op jit(solution)/shard_map/all_gather | solution.py:44
  404.4 3.0 fusion.11
  411.1 138.5 %all-reduce = bf16[64]{0:T(256)(128)(2,1)S(1)} all-reduce(bf16[64]{0:T(256)(128)(2,1)S(1)} %dynamic-update-slice), channel_id=1, replica_groups=mesh['ctx'=64,'fsdp'=8] {'ctx'}, use_global_device_ids=true, to_apply=%add | all-reduce | flops 64 | bytes 256
  549.6 10.8 %all-gather.9.cloned.1.call-done = bf16[256,128,128]{2,1,0:T(8,128)(2,1)} async-done(((bf16[4,128,128]{2,1,0:T(8,128)(2,1)}), bf16[256,128,128]{2,1,0:T(8,128)(2,1)}) %all-gather.9.cloned.1.call-update) | async-done | bytes 8388624 | tf_op jit(solution)/shard_map/all_gather | solution.py:12
  560.4 142.0 %while.12 = (s32[]{:T(128)}, f32[4,128,128]{2,1,0:T(8,128)S(1)}, s32[]{:T(128)}, bf16[64,4,128,128]{3,2,1,0:T(8,128)(2,1)}, bf16[64,1]{0,1:T(2,128)(2,1)S(1)}, /*index=5*/s32[]{:T(128)}, s32[]{:T(128)}, s32[]{:T(128)}) while((s32[]{:T(128)}, f32[4,128,128]{2,1,0:T(8,128)S(1)}, s32[]{:T(128)}, bf16[64,4,128,128]{3,2,1,0:T(8,128)(2,1)}, ...), condition=%wide.region_2.3_spmd, body=%wide.region_1.2_spmd.sunk | while | flops 196614 | bytes 655505 | solution.py:26
  561.1 1.6 convert_add_fusion.2
  563.3 1.6 convert_add_fusion.2
  565.6 1.6 convert_add_fusion.2
  567.8 1.6 convert_add_fusion.2
  570.1 1.6 convert_add_fusion.2
  572.3 1.6 convert_add_fusion.2
  574.6 1.6 convert_add_fusion.2
  576.8 1.6 convert_add_fusion.2
  579.1 1.6 convert_add_fusion.2
  581.3 1.6 convert_add_fusion.2
  583.6 1.6 convert_add_fusion.2
  585.8 1.6 convert_add_fusion.2
  588.1 1.6 convert_add_fusion.2
  590.3 1.6 convert_add_fusion.2
  592.6 1.6 convert_add_fusion.2
  610.6 1.6 convert_add_fusion.2
  612.9 1.6 convert_add_fusion.2
  630.9 1.6 convert_add_fusion.2
  633.2 1.6 convert_add_fusion.2
  653.4 1.6 convert_add_fusion.2
  655.7 1.6 convert_add_fusion.2
  673.7 1.6 convert_add_fusion.2
  676.0 1.6 convert_add_fusion.2
  696.2 1.6 convert_add_fusion.2
  698.5 1.6 convert_add_fusion.2
  (132 shorter events, 108.0 us)
Async XLA Ops:
  6.5 199.8 %copy-start = (bf16[1,128,4096]{2,1,0:T(8,128)(2,1)S(1)}, bf16[1,128,4096]{2,1,0:T(8,128)(2,1)}, u32[]{:S(2)}) copy-start(bf16[1,128,4096]{2,1,0:T(8,128)(2,1)} %param.8) | copy-start | bytes 3145732
  6.5 199.8 %all-gather.7.cloned.1.call-start = ((), (), s32[]{:S(2)}) async-start(), calls=%async_computation.1 | async-start | bytes 4202496 | tf_op jit(solution)/shard_map/all_gather | solution.py:45
  7.3 397.1 %all-gather.5.cloned.1.call-start = ((), (), s32[]{:S(2)}) async-start(), calls=%async_computation | async-start | bytes 4202496 | tf_op jit(solution)/shard_map/all_gather | solution.py:44
  8.0 552.4 %all-gather.9.cloned.1.call-start = ((), (), s32[]{:S(2)}) async-start(), calls=%async_computation.2 | async-start | bytes 8519680 | tf_op jit(solution)/shard_map/all_gather | solution.py:12
  209.3 199.7 %copy-start.1 = (bf16[1,128,512]{2,1,0:T(8,128)(2,1)S(1)}, bf16[1,128,512]{2,1,0:T(8,128)(2,1)}, u32[]{:S(2)}) copy-start(bf16[1,128,512]{2,1,0:T(8,128)(2,1)} %param.9) | copy-start | bytes 393220
  407.4 295.7 %copy-start.2 = (f32[512]{0:T(512)S(1)}, f32[512]{0:T(512)}, u32[]{:S(2)}) copy-start(f32[512]{0:T(512)} %param.13) | copy-start | bytes 6148
Sparse Core Ops, SparseCore 0:
  11.9 194.3 all-gather.6
  210.9 193.3 all-gather.4
  408.5 151.8 all-gather.8
where the time goes:
time: 712 us; the launch traced here: 711 us
  waiting for transfers between devices  403 us (57%)
  other arithmetic  142 us (20%)
  blocking collectives  138 us (19%)
  between operations  13.8 us (2%)
  matrix products  7.42 us (1%)
    all_gather x1, waiting for transfers between devices, on_device(): lax.all_gather(w_value, ('ctx', 'fsdp'), axis=0, tiled=True)  196 us
    all_gather x1, waiting for transfers between devices, on_device(): lax.all_gather(w_key, ('ctx', 'fsdp'), axis=0, tiled=True)  195 us
    unnamed x1, blocking collectives  138 us
    add x63, other arithmetic, combine(): return (jnp.maximum(earlier[0], later[0]), later[1] + keep * earlier[1])  104 us
    sub x63, other arithmetic, combine(): keep = 1.0 - later[0][0]  37.1 us
  transfers between devices with their start and end apart: 3, of which 3 were waited for; matrix products, arithmetic and copies ran while one was open for 1% of the time, Pallas kernels for 0%

commit v1 on v0

--- a/solution.py
+++ b/solution.py
@@ -36,13 +36,22 @@
 
 
 def on_device(tokens, queries, flags, w_key, w_value, norm_gain):
+
+    def _handle_boxes(my_data):
+        return jnp.concatenate(
+            lax.all_to_all(
+                jnp.stack([my_data] * lax.axis_size(("ctx", "fsdp"))), ("ctx", "fsdp"), 0, 0
+            ),
+            axis=0,
+        )
+
     rows = tokens[0]
     count = rows.shape[0]
     width = w_key.shape[1]
     heads = width // HEAD
     full_panels = (
         lax.all_gather(w_key, ("ctx", "fsdp"), axis=0, tiled=True),
-        lax.all_gather(w_value, ("ctx", "fsdp"), axis=0, tiled=True),
+        _handle_boxes(w_value),
     )
     proj_key = jnp.dot(rows, full_panels[0], preferred_element_type=jnp.float32)
     proj_value = jnp.dot(rows, full_panels[1], preferred_element_type=jnp.float32)

time: 712 us -> 574 us (0.81)
  waiting for transfers between devices: 403 us -> 239 us
  starting transfers between devices: 0.08 us -> 22.6 us
    all_gather x1 -> x0, waiting for transfers between devices: 196 us -> none  [on_device(): lax.all_gather(w_value, ('ctx', 'fsdp'), axis=0, tiled=True)]
    all_gather x1, waiting for transfers between devices: 195 us -> 229 us  [on_device(): lax.all_gather(w_key, ('ctx', 'fsdp'), axis=0, tiled=True)]
    all_to_all x0 -> x1, starting transfers between devices: none -> 22.5 us  [_handle_boxes(): lax.all_to_all(jnp.stack([my_data] * lax.axis_size(('ctx', 'fsdp'))), ('c...]
  transfers between devices with their start and end apart: 3 -> 3, of which waited for: 3 -> 2; matrix products, arithmetic and copies ran while one was open for 1% -> 1% of each run, Pallas kernels for 0% -> 0%
where the time goes in v1:
time: 574 us; the launch traced here: 572 us
  waiting for transfers between devices  239 us (42%)
  other arithmetic  142 us (25%)
  blocking collectives  139 us (24%)
  starting transfers between devices  22.6 us (4%)
  between operations  14.2 us (2%)
  matrix products  7.44 us (1%)
  local copies, waits for them, and re-layouts  6.86 us (1%)
    all_gather x1, waiting for transfers between devices, on_device(): lax.all_gather(w_key, ('ctx', 'fsdp'), axis=0, tiled=True)  229 us
    unnamed x1, blocking collectives  139 us
    add x63, other arithmetic, combine(): return (jnp.maximum(earlier[0], later[0]), later[1] + keep * earlier[1])  104 us
    sub x63, other arithmetic, combine(): keep = 1.0 - later[0][0]  37.1 us
    all_to_all x1, starting transfers between devices, _handle_boxes(): lax.all_to_all(jnp.stack([my_data] * lax.axis_size(('ctx', 'fsdp'))), ('c...  22.5 us
  transfers between devices with their start and end apart: 3, of which 2 were waited for; matrix products, arithmetic and copies ran while one was open for 1% of the time, Pallas kernels for 0%

profile of v1, /device:TPU:486, one launch (start us, length us, event | category | flops | bytes accessed | tf_op | source)
XLA Modules:
  0.0 572.1 jit_solution(2476046973694068867)
XLA Ops:
  6.5 3.0 stack.2
  9.6 22.5 %all-to-all-start = ((bf16[512,8,512]{2,1,0:T(8,128)(2,1)}), bf16[512,8,512]{2,1,0:T(8,128)(2,1)}, u32[]{:S(2)}, u32[]{:S(2)}) async-start(bf16[512,8,512]{2,1,0:T(8,128)(2,1)} %stack.2), calls=%async_computation | async-start | bytes 8388608 | tf_op jit(solution)/shard_map/all_to_all | solution.py:42
  34.4 228.5 %all-gather.4.cloned.1.call-done = bf16[4096,512]{1,0:T(8,128)(2,1)} async-done(((bf16[8,512]{1,0:T(8,128)(2,1)}), bf16[4096,512]{1,0:T(8,128)(2,1)}) %all-gather.4.cloned.1.call-update) | async-done | bytes 4194320 | tf_op jit(solution)/shard_map/all_gather | solution.py:53
  263.0 3.0 fusion.16
  266.1 2.9 fusion.4
  272.9 138.6 %all-reduce = bf16[64]{0:T(256)(128)(2,1)S(1)} all-reduce(bf16[64]{0:T(256)(128)(2,1)S(1)} %dynamic-update-slice), channel_id=1, replica_groups=mesh['ctx'=64,'fsdp'=8] {'ctx'}, use_global_device_ids=true, to_apply=%add | all-reduce | flops 64 | bytes 256
  411.5 10.2 %all-gather.6.cloned.1.call-done = bf16[256,128,128]{2,1,0:T(8,128)(2,1)} async-done(((bf16[4,128,128]{2,1,0:T(8,128)(2,1)}), bf16[256,128,128]{2,1,0:T(8,128)(2,1)}) %all-gather.6.cloned.1.call-update) | async-done | bytes 8388624 | tf_op jit(solution)/shard_map/all_gather | solution.py:12
  421.7 142.0 %while.12 = (s32[]{:T(128)}, f32[4,128,128]{2,1,0:T(8,128)S(1)}, s32[]{:T(128)}, bf16[64,4,128,128]{3,2,1,0:T(8,128)(2,1)}, bf16[64,1]{0,1:T(2,128)(2,1)S(1)}, /*index=5*/s32[]{:T(128)}, s32[]{:T(128)}, s32[]{:T(128)}) while((s32[]{:T(128)}, f32[4,128,128]{2,1,0:T(8,128)S(1)}, s32[]{:T(128)}, bf16[64,4,128,128]{3,2,1,0:T(8,128)(2,1)}, ...), condition=%wide.region_2.3_spmd, body=%wide.region_1.2_spmd.sunk | while | flops 196614 | bytes 655505 | solution.py:26
  422.3 1.6 convert_add_fusion.2
  424.6 1.6 convert_add_fusion.2
  426.9 1.6 convert_add_fusion.2
  429.1 1.6 convert_add_fusion.2
  431.4 1.6 convert_add_fusion.2
  433.6 1.6 convert_add_fusion.2
  435.9 1.6 convert_add_fusion.2
  438.1 1.6 convert_add_fusion.2
  440.4 1.6 convert_add_fusion.2
  442.6 1.6 convert_add_fusion.2
  444.9 1.6 convert_add_fusion.2
  447.1 1.6 convert_add_fusion.2
  449.4 1.6 convert_add_fusion.2
  451.6 1.6 convert_add_fusion.2
  460.7 1.6 convert_add_fusion.2
  462.9 1.6 convert_add_fusion.2
  483.2 1.6 convert_add_fusion.2
  485.4 1.6 convert_add_fusion.2
  503.5 1.6 convert_add_fusion.2
  505.7 1.6 convert_add_fusion.2
  526.0 1.6 convert_add_fusion.2
  528.2 1.6 convert_add_fusion.2
  546.3 1.6 convert_add_fusion.2
  548.5 1.6 convert_add_fusion.2
  (134 shorter events, 108.5 us)
Async XLA Ops:
  6.5 256.4 %copy-start = (bf16[1,128,4096]{2,1,0:T(8,128)(2,1)S(1)}, bf16[1,128,4096]{2,1,0:T(8,128)(2,1)}, u32[]{:S(2)}) copy-start(bf16[1,128,4096]{2,1,0:T(8,128)(2,1)} %param.8) | copy-start | bytes 3145732
  9.6 23.3 %copy-start.3 = (s32[1,128]{1,0:T(1,128)S(1)}, s32[1,128]{1,0:T(1,128)}, u32[]{:S(2)}) copy-start(s32[1,128]{1,0:T(1,128)} %param.10) | copy-start | bytes 1540
  9.6 256.6 %all-to-all-start = ((bf16[512,8,512]{2,1,0:T(8,128)(2,1)}), bf16[512,8,512]{2,1,0:T(8,128)(2,1)}, u32[]{:S(2)}, u32[]{:S(2)}) async-start(bf16[512,8,512]{2,1,0:T(8,128)(2,1)} %stack.2), calls=%async_computation | async-start | bytes 8388608 | tf_op jit(solution)/shard_map/all_to_all | solution.py:42
  32.0 230.9 %all-gather.4.cloned.1.call-start = ((), (), s32[]{:S(2)}) async-start(), calls=%async_computation.1 | async-start | bytes 4202496 | tf_op jit(solution)/shard_map/all_gather | solution.py:53
  32.8 388.9 %all-gather.6.cloned.1.call-start = ((), (), s32[]{:S(2)}) async-start(), calls=%async_computation.2 | async-start | bytes 8519680 | tf_op jit(solution)/shard_map/all_gather | solution.py:12
  266.0 4.7 copy-start.1
  269.0 295.3 %copy-start.2 = (f32[512]{0:T(512)S(1)}, f32[512]{0:T(512)}, u32[]{:S(2)}) copy-start(f32[512]{0:T(512)} %param.13) | copy-start | bytes 6148
Sparse Core Ops, SparseCore 0:
  37.5 225.4 all-gather.3
  270.2 151.4 all-gather.5
